TPU v7x, 32 devices: a whole 2x2x4 slice. The times are simulated.
32 devices in a mesh: fsdp: 8 (over z, y), tp: 4 (over x, core).
Axes of the slice: x: 2, y: 2, z: 4, core: 2. Of those that a mesh axis runs over, the one named last changes fastest.
Arguments:
- inputs: bfloat16 [4096, 1024], P(('fsdp', 'tp')), may hold values from -6 to 6
- cotangent: bfloat16 [4096, 1024], P(('fsdp', 'tp')), may hold values from -6 to 6
- lengths: int32 [8, 8], P('fsdp'), may hold values from 1 to 256, 512 in all within a row
- qkv_weight: bfloat16 [2, 3, 1024, 1024], P(None, None, 'fsdp', 'tp'), as said below
- qv_bias: bfloat16 [2, 2, 1024], P(None, None, ('tp', 'fsdp')), may hold values from -3 to 3
- out_weight: bfloat16 [2, 1024, 1024], P(None, 'tp', 'fsdp'), may hold values from -1 to 1
- fc_weight: bfloat16 [2, 1024, 4096], P(None, 'fsdp', 'tp'), may hold values from -0.1875 to 0.1875
- fc_bias: bfloat16 [2, 4096], P(None, ('tp', 'fsdp')), may hold values from -3 to 3
- proj_weight: bfloat16 [2, 4096, 1024], P(None, 'tp', 'fsdp'), may hold values from -0.09375 to 0.09375
- norm_gains: float32 [2, 2, 1024], P(None, None, ('fsdp', 'tp')), may hold values from 0.25 to 1.75
- shifts: float32 [2, 4, 1024], P(None, None, ('fsdp', 'tp')), may hold values from -3 to 3
Outputs:
- out_acts: bfloat16 [4096, 1024], P(('fsdp', 'tp'))
- in_grad: float32 [4096, 1024], P(('fsdp', 'tp'))
- qkv_grad: float32 [2, 3, 1024, 1024], P(None, None, 'fsdp', 'tp')
- qv_bias_grad: float32 [2, 2, 1024], P(None, None, ('tp', 'fsdp'))
- out_grad: float32 [2, 1024, 1024], P(None, 'tp', 'fsdp')
- fc_grad: float32 [2, 1024, 4096], P(None, 'fsdp', 'tp')
- fc_bias_grad: float32 [2, 4096], P(None, ('tp', 'fsdp'))
- proj_grad: float32 [2, 4096, 1024], P(None, 'tp', 'fsdp')
- gains_grad: float32 [2, 2, 1024], P(None, None, ('fsdp', 'tp'))
- shifts_grad: float32 [2, 4, 1024], P(None, None, ('fsdp', 'tp'))
Inputs may be any that keep to these rules, and one draw needn't show every extreme that they name: Row g holds the lengths of group g's sequences in row order; they sum to 512 and the longest is 256. `qkv_weight`: columns h * 64 to (h + 1) * 64 - 1 of each projection belong to head h. Every entry lies between -6 / sqrt(1024) and 6 / sqrt(1024).
All inputs are finite; a program needn't handle non-finite values.
Results may differ from a plain program's by a relative error of at most 0.023.
Values may be sent and summed in bfloat16 or wider, within the bound.
No kernel may reach another device: no remote copies, remote signals or barrier semaphores. Data moves between devices by JAX's collectives and lax.ppermute only.
A program may use at most 128 MiB of HBM per device.

v0:
```python
import jax
import jax.numpy as jnp
from jax import lax
from jax.sharding import PartitionSpec as P

HEAD_DIM = 64
LAYERS = 2
eps_norm = 1e-05


def norm_stats(values):
    centre = values - jnp.mean(values, axis=-1, keepdims=True)
    variance = jnp.mean(centre * centre, axis=-1, keepdims=True)
    inv_std = lax.rsqrt(variance + eps_norm)
    return (centre * inv_std, inv_std)


def norm_back(d_normed, normed, inv_std):
    return inv_std * (
        d_normed
        - jnp.mean(d_normed, axis=-1, keepdims=True)
        - normed * jnp.mean(d_normed * normed, axis=-1, keepdims=True)
    )


def gelu_tanh(values):
    return jax.nn.gelu(values, approximate=True)


def gelu_back(pre_act, d_act):
    return jax.vjp(gelu_tanh, pre_act)[1](d_act)[0]


def allowed_pairs(seq_lens, group_len):
    bounds = jnp.cumsum(seq_lens)
    positions = jnp.arange(group_len, dtype=jnp.int32)
    segment = jnp.sum((positions[:, None] >= bounds[None, :]).astype(jnp.int32), axis=1)
    return (segment[:, None] == segment[None, :]) & (positions[None, :] <= positions[:, None])


def head_split(values):
    return values.reshape(values.shape[0], -1, HEAD_DIM)


def scores_of(queries, keys_in, allowed):
    raw = jnp.einsum(
        "qhd,khd->hqk", head_split(queries), head_split(keys_in), preferred_element_type=jnp.float32
    ) * HEAD_DIM ** (-0.5)
    return jnp.where(allowed[None], raw, -1e30)


def attend(queries, keys_in, values_in, allowed):
    scores = scores_of(queries, keys_in, allowed)
    row_top = jnp.max(scores, axis=-1)
    log_total = row_top + jnp.log(jnp.sum(jnp.exp(scores - row_top[..., None]), axis=-1))
    prob_low = jnp.exp(scores - log_total[..., None]).astype(jnp.bfloat16)
    mixed_heads = jnp.einsum(
        "hqk,khd->qhd", prob_low, head_split(values_in), preferred_element_type=jnp.float32
    )
    return (mixed_heads.reshape(mixed_heads.shape[0], -1).astype(jnp.bfloat16), log_total)


def attend_back(queries, keys_in, values_in, mixed_heads, log_total, d_mixed, allowed):
    scores = scores_of(queries, keys_in, allowed)
    probs = jnp.exp(scores - log_total[..., None])
    prob_low = probs.astype(jnp.bfloat16)
    dm_heads = head_split(d_mixed)
    d_values = jnp.einsum("hqk,qhd->khd", prob_low, dm_heads, preferred_element_type=jnp.float32)
    d_probs = jnp.einsum(
        "qhd,khd->hqk", dm_heads, head_split(values_in), preferred_element_type=jnp.float32
    )
    row_dot = jnp.transpose(
        jnp.sum(head_split(mixed_heads).astype(jnp.float32) * dm_heads.astype(jnp.float32), axis=-1)
    )
    d_scores = (probs * (d_probs - row_dot[:, :, None])).astype(jnp.bfloat16)
    scale = HEAD_DIM ** (-0.5)
    d_queries = (
        jnp.einsum(
            "hqk,khd->qhd", d_scores, head_split(keys_in), preferred_element_type=jnp.float32
        )
        * scale
    )
    d_keys = (
        jnp.einsum(
            "hqk,qhd->khd", d_scores, head_split(queries), preferred_element_type=jnp.float32
        )
        * scale
    )
    group_len = queries.shape[0]
    return (
        d_queries.reshape(group_len, -1),
        d_keys.reshape(group_len, -1),
        d_values.reshape(group_len, -1),
    )


def gather_acts(values):
    return lax.all_gather(values, "tp", axis=0, tiled=True)


def gather_grads(values):
    return lax.all_gather(values, "tp", axis=0, tiled=True)


def sum_branch(partial_fn, tok_rows):
    return lax.psum_scatter(
        partial_fn(jnp.int32(0), tok_rows * lax.axis_size("tp")),
        "tp",
        scatter_dimension=0,
        tiled=True,
    )


def sum_inputs(partial_fn, tok_rows):
    return lax.psum_scatter(
        partial_fn(jnp.int32(0), tok_rows * lax.axis_size("tp")).astype(jnp.bfloat16),
        "tp",
        scatter_dimension=0,
        tiled=True,
    ).astype(jnp.float32)


def contract_first(left, right):
    return lax.dot_general(
        left, right, (((0,), (0,)), ((), ())), preferred_element_type=jnp.float32
    )


def contract_last(left, right):
    return lax.dot_general(
        left, right, (((1,), (1,)), ((), ())), preferred_element_type=jnp.float32
    )


def body(
    inputs,
    cotangent,
    lengths,
    qkv_weight,
    qv_bias,
    out_weight,
    fc_weight,
    fc_bias,
    proj_weight,
    norm_gains,
    shifts,
):
    tok_rows = inputs.shape[0]
    group_len = tok_rows * lax.axis_size("tp")
    gains_all, shifts_all = (
        lax.all_gather(norm_gains, ("fsdp", "tp"), axis=2, tiled=True),
        lax.all_gather(shifts, ("fsdp", "tp"), axis=2, tiled=True),
    )
    allowed = allowed_pairs(lengths[0], group_len)
    residual = inputs.astype(jnp.float32)
    saved_acts = []
    for layer_id in range(LAYERS):
        weights = (
            lax.all_gather(qkv_weight[layer_id], "fsdp", axis=1, tiled=True),
            lax.all_gather(out_weight[layer_id], "fsdp", axis=1, tiled=True),
            lax.all_gather(fc_weight[layer_id], "fsdp", axis=0, tiled=True),
            lax.all_gather(proj_weight[layer_id], "fsdp", axis=1, tiled=True),
            lax.all_gather(qv_bias[layer_id], "fsdp", axis=1, tiled=True),
            lax.all_gather(fc_bias[layer_id], "fsdp", axis=0, tiled=True),
        )
        w_qkv, w_out, w_fc, w_proj, b_qv, b_fc = weights
        norm_gain = gains_all[layer_id]
        offset_rows = shifts_all[layer_id]
        normed_one, inv_one = norm_stats(residual)
        act_one = gather_acts((normed_one * norm_gain[0] + offset_rows[0]).astype(jnp.bfloat16))
        bias_rows = jnp.stack(
            [
                b_qv[0].astype(jnp.float32),
                jnp.zeros(b_qv[0].shape, jnp.float32),
                b_qv[1].astype(jnp.float32),
            ]
        )
        projected = (
            jnp.einsum("gd,cdh->cgh", act_one, w_qkv, preferred_element_type=jnp.float32)
            + bias_rows[:, None, :]
        )
        projected = projected.astype(jnp.bfloat16)
        mixed_heads, log_total = attend(projected[0], projected[1], projected[2], allowed)

        def out_part(first_row, row_count, mixed_heads=mixed_heads, w_out=w_out):
            return jnp.dot(mixed_heads, w_out, preferred_element_type=jnp.float32)

        middle = residual + sum_branch(out_part, tok_rows) + offset_rows[2]
        normed_two, inv_two = norm_stats(middle)
        act_two = gather_acts((normed_two * norm_gain[1] + offset_rows[1]).astype(jnp.bfloat16))
        pre_act = jnp.dot(act_two, w_fc, preferred_element_type=jnp.float32) + b_fc.astype(
            jnp.float32
        )
        hidden = gelu_tanh(pre_act).astype(jnp.bfloat16)

        def mlp_part(first_row, row_count, hidden=hidden, w_proj=w_proj):
            return jnp.dot(hidden, w_proj, preferred_element_type=jnp.float32)

        after_block = middle + sum_branch(mlp_part, tok_rows) + offset_rows[3]
        saved_acts.append(
            (residual, act_one, projected, mixed_heads, log_total, middle, act_two, pre_act, hidden)
        )
        residual = after_block
    out_rows = residual.astype(jnp.bfloat16)
    d_res = cotangent.astype(jnp.float32)
    gain_list = [None] * LAYERS
    shift_list = [None] * LAYERS
    grad_list = [None] * LAYERS
    for layer_id in reversed(range(LAYERS)):
        weights = (
            lax.all_gather(qkv_weight[layer_id], "fsdp", axis=1, tiled=True),
            lax.all_gather(out_weight[layer_id], "fsdp", axis=1, tiled=True),
            lax.all_gather(fc_weight[layer_id], "fsdp", axis=0, tiled=True),
            lax.all_gather(proj_weight[layer_id], "fsdp", axis=1, tiled=True),
            lax.all_gather(qv_bias[layer_id], "fsdp", axis=1, tiled=True),
            lax.all_gather(fc_bias[layer_id], "fsdp", axis=0, tiled=True),
        )
        w_qkv, w_out, w_fc, w_proj, b_qv, b_fc = weights
        norm_gain = gains_all[layer_id]
        residual, act_one, projected, mixed_heads, log_total, middle, act_two, pre_act, hidden = (
            saved_acts[layer_id]
        )
        d_after = d_res
        d_low = gather_grads(d_after.astype(jnp.bfloat16))
        d_proj = contract_first(hidden, d_low)
        d_hidden = contract_last(d_low, w_proj)
        d_pre = gelu_back(pre_act, d_hidden)
        d_pre_low = d_pre.astype(jnp.bfloat16)
        d_fc = contract_first(act_two, d_pre_low)
        d_fc_bias = jnp.sum(d_pre, axis=0)

        def fc_part(first_row, row_count, d_pre_low=d_pre_low, w_fc=w_fc):
            return contract_last(d_pre_low, w_fc)

        d_act_two = sum_inputs(fc_part, tok_rows)
        normed_two, inv_two = norm_stats(middle)
        d_middle = d_after + norm_back(d_act_two * norm_gain[1], normed_two, inv_two)
        d_mid_low = gather_grads(d_middle.astype(jnp.bfloat16))
        d_out = contract_first(mixed_heads, d_mid_low)
        d_mixed = contract_last(d_mid_low, w_out).astype(jnp.bfloat16)
        d_queries, d_keys, d_values = attend_back(
            projected[0], projected[1], projected[2], mixed_heads, log_total, d_mixed, allowed
        )
        d_bias = jnp.stack([jnp.sum(d_queries, axis=0), jnp.sum(d_values, axis=0)])
        d_proj_low = jnp.stack([d_queries, d_keys, d_values]).astype(jnp.bfloat16)
        d_qkv = jnp.einsum("gd,cgh->cdh", act_one, d_proj_low, preferred_element_type=jnp.float32)

        def qkv_part(first_row, row_count, d_proj_low=d_proj_low, w_qkv=w_qkv):
            return jnp.einsum("cgh,cdh->gd", d_proj_low, w_qkv, preferred_element_type=jnp.float32)

        d_act_one = sum_inputs(qkv_part, tok_rows)
        normed_one, inv_one = norm_stats(residual)
        d_res = d_middle + norm_back(d_act_one * norm_gain[0], normed_one, inv_one)
        gain_list[layer_id] = jnp.stack(
            [jnp.sum(d_act_one * normed_one, axis=0), jnp.sum(d_act_two * normed_two, axis=0)]
        )
        shift_list[layer_id] = jnp.stack(
            [
                jnp.sum(d_act_one, axis=0),
                jnp.sum(d_act_two, axis=0),
                jnp.sum(d_middle, axis=0),
                jnp.sum(d_after, axis=0),
            ]
        )
        layer_grads = (d_qkv, d_bias, d_out, d_fc, d_fc_bias, d_proj)
        grad_list[layer_id] = (
            lax.psum_scatter(
                layer_grads[0].astype(jnp.bfloat16), "fsdp", scatter_dimension=1, tiled=True
            ).astype(jnp.float32),
            lax.psum_scatter(
                layer_grads[1].astype(jnp.bfloat16), "fsdp", scatter_dimension=1, tiled=True
            ).astype(jnp.float32),
            lax.psum_scatter(
                layer_grads[2].astype(jnp.bfloat16), "fsdp", scatter_dimension=1, tiled=True
            ).astype(jnp.float32),
            lax.psum_scatter(
                layer_grads[3].astype(jnp.bfloat16), "fsdp", scatter_dimension=0, tiled=True
            ).astype(jnp.float32),
            lax.psum_scatter(
                layer_grads[4].astype(jnp.bfloat16), "fsdp", scatter_dimension=0, tiled=True
            ).astype(jnp.float32),
            lax.psum_scatter(
                layer_grads[5].astype(jnp.bfloat16), "fsdp", scatter_dimension=1, tiled=True
            ).astype(jnp.float32),
        )
    stacked = tuple(
        (
            jnp.stack([grad_list[layer_id][member] for layer_id in range(LAYERS)])
            for member in range(6)
        )
    )
    gains_grad, shifts_grad = (
        lax.psum_scatter(jnp.stack(gain_list), ("fsdp", "tp"), scatter_dimension=2, tiled=True),
        lax.psum_scatter(jnp.stack(shift_list), ("fsdp", "tp"), scatter_dimension=2, tiled=True),
    )
    return (
        out_rows,
        d_res,
        stacked[0],
        stacked[1],
        stacked[2],
        stacked[3],
        stacked[4],
        stacked[5],
        gains_grad,
        shifts_grad,
    )


def solution(mesh):
    in_specs = (
        P(("fsdp", "tp"), None),
        P(("fsdp", "tp"), None),
        P("fsdp", None),
        P(None, None, "fsdp", "tp"),
        P(None, None, ("tp", "fsdp")),
        P(None, "tp", "fsdp"),
        P(None, "fsdp", "tp"),
        P(None, ("tp", "fsdp")),
        P(None, "tp", "fsdp"),
        P(None, None, ("fsdp", "tp")),
        P(None, None, ("fsdp", "tp")),
    )
    out_specs = (
        P(("fsdp", "tp"), None),
        P(("fsdp", "tp"), None),
        P(None, None, "fsdp", "tp"),
        P(None, None, ("tp", "fsdp")),
        P(None, "tp", "fsdp"),
        P(None, "fsdp", "tp"),
        P(None, ("tp", "fsdp")),
        P(None, "tp", "fsdp"),
        P(None, None, ("fsdp", "tp")),
        P(None, None, ("fsdp", "tp")),
    )
    return jax.shard_map(body, mesh=mesh, in_specs=in_specs, out_specs=out_specs, check_vma=False)
```

profile of v0, /device:TPU:0, one launch (start us, length us, event | category | flops | bytes accessed | tf_op | source)
XLA Modules:
  0.0 1883.8 jit_solution(10463837423635150273)
XLA Ops:
  8.0 46.2 %all_gather.75 = f32[2,4,1024]{1,0,2:T(2,128)S(1)} all-gather(f32[2,4,32]{1,0,2:T(2,128)S(1)} %copy.99), channel_id=1, replica_groups=mesh['fsdp'=8,'tp'=4] {'fsdp','tp'}, dimensions={2}, use_global_device_ids=true | all-gather | bytes 33792 | tf_op jit(solution)/shard_map/all_gather | solution.py:152
  54.2 27.1 %slice_reduce_fusion = (f32[1024]{0:T(1024)S(1)}, f32[1024]{0:T(1024)S(1)}, f32[1024]{0:T(1024)S(1)}, f32[1024]{0:T(1024)S(1)}, f32[1024]{0:T(1024)S(1)}, /*inde...) fusion(f32[2,4,1024]{1,0,2:T(2,128)S(1)} %all_gather.75), kind=kLoop, calls=%fused_computation.148 | loop fusion | bytes 65536 | tf_op jit(solution)/shard_map/slice | solution.py:199
  81.5 40.1 %all_gather.74 = f32[2,2,1024]{1,0,2:T(2,128)S(1)} all-gather(f32[2,2,32]{1,0,2:T(2,128)S(1)} %copy.98), channel_id=1, replica_groups=mesh['fsdp'=8,'tp'=4] {'fsdp','tp'}, dimensions={2}, use_global_device_ids=true | all-gather | bytes 16896 | tf_op jit(solution)/shard_map/all_gather | solution.py:151
  121.6 26.0 %slice_reduce_fusion.2 = (f32[1024]{0:T(1024)S(1)}, f32[1024]{0:T(1024)S(1)}, f32[1024]{0:T(1024)S(1)}, f32[1024]{0:T(1024)S(1)}) fusion(f32[2,2,1024]{1,0,2:T(2,128)S(1)} %all_gather.74), kind=kLoop, calls=%fused_computation.150 | loop fusion | bytes 32768 | tf_op jit(solution)/shard_map/slice | solution.py:190
  150.4 30.7 %all-gather.1 = bf16[1,2,256]{1,0,2:T(2,128)(2,1)S(1)} all-gather(bf16[1,2,32]{1,0,2:T(2,128)(2,1)S(1)} %copy.160), channel_id=3, replica_groups=mesh['fsdp'=8,'tp'=4] {'fsdp'}, dimensions={2}, use_global_device_ids=true | all-gather | bytes 1152 | tf_op jit(solution)/shard_map/all_gather | solution.py:163
  181.2 31.3 %all-gather.7 = bf16[1,2,256]{1,0,2:T(2,128)(2,1)S(1)} all-gather(bf16[1,2,32]{1,0,2:T(2,128)(2,1)S(1)} %copy.162), channel_id=9, replica_groups=mesh['fsdp'=8,'tp'=4] {'fsdp'}, dimensions={2}, use_global_device_ids=true | all-gather | bytes 1152 | tf_op jit(solution)/shard_map/all_gather | solution.py:163
  219.8 27.0 %all-gather.2 = bf16[1,256,1024]{2,1,0:T(8,128)(2,1)S(1)} all-gather(bf16[1,256,128]{2,1,0:T(8,128)(2,1)S(1)} %get-tuple-element.119), channel_id=4, replica_groups=mesh['fsdp'=8,'tp'=4] {'fsdp'}, dimensions={2}, use_global_device_ids=true | all-gather | bytes 589824 | tf_op jit(solution)/shard_map/all_gather | solution.py:160
  256.9 27.6 %reduce-scatter.41.cloned.1.call-done = f32[128,1024]{1,0:T(8,128)} async-done(((f32[512,1024]{1,0:T(8,128)}), f32[128,1024]{1,0:T(8,128)}) %reduce-scatter.41.cloned.1.call-update) | async-done | bytes 524304 | tf_op jit(solution)/shard_map/reduce_scatter | solution.py:106
  287.8 20.6 %all-gather.4 = bf16[1,1024]{1,0:T(2,128)(2,1)S(1)} all-gather(bf16[1,128]{1,0:T(2,128)(2,1)S(1)} %get-tuple-element.123), channel_id=6, replica_groups=mesh['fsdp'=8,'tp'=4] {'fsdp'}, dimensions={1}, use_global_device_ids=true | all-gather | bytes 2304 | tf_op jit(solution)/shard_map/all_gather | solution.py:164
  308.4 27.9 %all-gather.45.cloned.1.call-done = bf16[1,1024,1024]{2,1,0:T(8,128)(2,1)} async-done(((bf16[1,128,1024]{2,1,0:T(8,128)(2,1)}), bf16[1,1024,1024]{2,1,0:T(8,128)(2,1)}) %all-gather.45.cloned.1.call-update) | async-done | bytes 2097168 | tf_op jit(solution)/shard_map/all_gather | solution.py:161
  336.3 17.2 all-gather.29.cloned.1.call-done
  353.5 4.6 fusion.30
  358.1 48.3 %all-gather.47.cloned.1.call-done = bf16[1,1024,1024]{2,1,0:T(8,128)(2,1)} async-done(((bf16[1,1024,128]{2,1,0:T(8,128)(2,1)}), bf16[1,1024,1024]{2,1,0:T(8,128)(2,1)}) %all-gather.47.cloned.1.call-update) | async-done | bytes 2097168 | tf_op jit(solution)/shard_map/all_gather | solution.py:162
  406.4 5.1 fusion.26
  412.6 28.4 %reduce-scatter.43.cloned.1.call-done = f32[128,1024]{1,0:T(8,128)} async-done(((f32[512,1024]{1,0:T(8,128)}), f32[128,1024]{1,0:T(8,128)}) %reduce-scatter.43.cloned.1.call-update) | async-done | bytes 524304 | tf_op jit(solution)/shard_map/reduce_scatter | solution.py:106
  443.4 29.3 %all-gather.8 = bf16[1,256,1024]{2,1,0:T(8,128)(2,1)S(1)} all-gather(bf16[1,256,128]{2,1,0:T(8,128)(2,1)S(1)} %get-tuple-element.118), channel_id=10, replica_groups=mesh['fsdp'=8,'tp'=4] {'fsdp'}, dimensions={2}, use_global_device_ids=true | all-gather | bytes 589824 | tf_op jit(solution)/shard_map/all_gather | solution.py:160
  472.7 19.6 %all-gather.49.cloned.1.call-done = bf16[1,3,1024,256]{2,3,1,0:T(8,128)(2,1)} async-done(((bf16[1,3,128,256]{2,3,1,0:T(8,128)(2,1)}), bf16[1,3,1024,256]{2,3,1,0:T(8,128)(2,1)}) %all-gather.49.cloned.1.call-update) | async-done | bytes 1572880 | tf_op jit(solution)/shard_map/all_gather | solution.py:159
  492.3 17.1 all-gather.31.cloned.1.call-done
  519.0 30.5 %reduce-scatter.45.cloned.1.call-done = f32[128,1024]{1,0:T(8,128)} async-done(((f32[512,1024]{1,0:T(8,128)}), f32[128,1024]{1,0:T(8,128)}) %reduce-scatter.45.cloned.1.call-update) | async-done | bytes 524304 | tf_op jit(solution)/shard_map/reduce_scatter | solution.py:106
  553.2 20.6 %all-gather.10 = bf16[1,1024]{1,0:T(2,128)(2,1)S(1)} all-gather(bf16[1,128]{1,0:T(2,128)(2,1)S(1)} %get-tuple-element.122), channel_id=12, replica_groups=mesh['fsdp'=8,'tp'=4] {'fsdp'}, dimensions={1}, use_global_device_ids=true | all-gather | bytes 2304 | tf_op jit(solution)/shard_map/all_gather | solution.py:164
  573.9 27.6 %all-gather.51.cloned.1.call-done = bf16[1,1024,1024]{2,1,0:T(8,128)(2,1)} async-done(((bf16[1,128,1024]{2,1,0:T(8,128)(2,1)}), bf16[1,1024,1024]{2,1,0:T(8,128)(2,1)}) %all-gather.51.cloned.1.call-update) | async-done | bytes 2097168 | tf_op jit(solution)/shard_map/all_gather | solution.py:161
  601.5 17.3 all-gather.33.cloned.1.call-done
  618.7 4.5 fusion.22
  623.2 13.8 all-gather.35.cloned.1.call-done
  637.0 52.9 %all-gather.53.cloned.1.call-done = bf16[1,1024,1024]{2,1,0:T(8,128)(2,1)} async-done(((bf16[1,1024,128]{2,1,0:T(8,128)(2,1)}), bf16[1,1024,1024]{2,1,0:T(8,128)(2,1)}) %all-gather.53.cloned.1.call-update) | async-done | bytes 2097168 | tf_op jit(solution)/shard_map/all_gather | solution.py:162
  689.9 5.2 fusion.151
  698.4 5.1 fusion.18
  703.9 17.5 reduce-scatter.49.cloned.1.call-done
  722.7 32.3 %reduce-scatter.47.cloned.1.call-done = f32[128,1024]{1,0:T(8,128)} async-done(((f32[512,1024]{1,0:T(8,128)}), f32[128,1024]{1,0:T(8,128)}) %reduce-scatter.47.cloned.1.call-update) | async-done | bytes 524304 | tf_op jit(solution)/shard_map/reduce_scatter | solution.py:106
  758.0 16.8 all-gather.37.cloned.1.call-done
  789.7 24.9 %reduce-scatter.51.cloned.1.call-done = bf16[128,1024]{1,0:T(8,128)(2,1)} async-done(((bf16[512,1024]{1,0:T(8,128)(2,1)}), bf16[128,1024]{1,0:T(8,128)(2,1)}) %reduce-scatter.51.cloned.1.call-update) | async-done | bytes 262160 | tf_op jit(solution)/shard_map/reduce_scatter | solution.py:115
  817.8 16.8 all-gather.39.cloned.1.call-done
  834.6 5.2 fusion.152
  843.2 24.9 %reduce-scatter.53.cloned.1.call-done = bf16[128,1024]{1,0:T(8,128)(2,1)} async-done(((bf16[512,1024]{1,0:T(8,128)(2,1)}), bf16[128,1024]{1,0:T(8,128)(2,1)}) %reduce-scatter.53.cloned.1.call-update) | async-done | bytes 262160 | tf_op jit(solution)/shard_map/reduce_scatter | solution.py:115
  871.5 16.6 all-gather.41.cloned.1.call-done
  951.2 47.0 %reduce-scatter.75.cloned.1.call-done = bf16[128,1024]{1,0:T(8,128)(2,1)} async-done(((bf16[1024,1024]{1,0:T(8,128)(2,1)}), bf16[128,1024]{1,0:T(8,128)(2,1)}) %reduce-scatter.75.cloned.1.call-update) | async-done | bytes 262160
  999.4 63.6 %reduce-scatter.67.cloned.1.call-done = bf16[32,2]{1,0:T(8,128)(2,1)} async-done(((bf16[256,2]{1,0:T(8,128)(2,1)}), bf16[32,2]{1,0:T(8,128)(2,1)}) %reduce-scatter.67.cloned.1.call-update) | async-done | bytes 144
  1063.8 64.8 %reduce-scatter.71.cloned.1.call-done = bf16[128,256]{1,0:T(8,128)(2,1)} async-done(((bf16[1024,256]{1,0:T(8,128)(2,1)}), bf16[128,256]{1,0:T(8,128)(2,1)}) %reduce-scatter.71.cloned.1.call-update) | async-done | bytes 65552
  1129.5 66.8 %reduce-scatter.63.cloned.1.call-done = bf16[128,768]{1,0:T(8,128)(2,1)} async-done(((bf16[1024,768]{1,0:T(8,128)(2,1)}), bf16[128,768]{1,0:T(8,128)(2,1)}) %reduce-scatter.63.cloned.1.call-update) | async-done | bytes 196624
  1197.5 19.1 %all-reduce.2 = (bf16[1024]{0:T(1024)(128)(2,1)S(1)}, bf16[1024]{0:T(1024)(128)(2,1)S(1)}) all-reduce(bf16[1024]{0:T(1024)(128)(2,1)S(1)} %get-tuple-element.138, bf16[1024]{0:T(1024)(128)(2,1)S(1)} %get-tuple-element.140), channel_id=31, replica_groups=mesh['fsdp'=8,'tp'=4] {'fsdp'}, use_global_device_ids=true, to_apply=%region_47.48.clone | all-reduce | flops 2048 | bytes 8192
  1217.4 43.6 %reduce-scatter.65.cloned.1.call-done = bf16[32,2]{1,0:T(8,128)(2,1)} async-done(((bf16[256,2]{1,0:T(8,128)(2,1)}), bf16[32,2]{1,0:T(8,128)(2,1)}) %reduce-scatter.65.cloned.1.call-update) | async-done | bytes 144
  1262.3 69.5 %reduce-scatter.73.cloned.1.call-done = bf16[128,1024]{1,0:T(8,128)(2,1)} async-done(((bf16[1024,1024]{1,0:T(8,128)(2,1)}), bf16[128,1024]{1,0:T(8,128)(2,1)}) %reduce-scatter.73.cloned.1.call-update) | async-done | bytes 262160
  1334.0 68.7 %reduce-scatter.59.cloned.1.call-done = bf16[128,1024]{1,0:T(8,128)(2,1)} async-done(((bf16[1024,1024]{1,0:T(8,128)(2,1)}), bf16[128,1024]{1,0:T(8,128)(2,1)}) %reduce-scatter.59.cloned.1.call-update) | async-done | bytes 262160 | tf_op jit(solution)/shard_map/reduce_scatter | solution.py:276
  1402.7 70.5 %reduce-scatter.57.cloned.1.call-done = bf16[128,1024]{1,0:T(8,128)(2,1)} async-done(((bf16[1024,1024]{1,0:T(8,128)(2,1)}), bf16[128,1024]{1,0:T(8,128)(2,1)}) %reduce-scatter.57.cloned.1.call-update) | async-done | bytes 262160 | tf_op jit(solution)/shard_map/reduce_scatter | solution.py:276
  1475.2 63.6 %reduce-scatter.69.cloned.1.call-done = bf16[128,256]{1,0:T(8,128)(2,1)} async-done(((bf16[1024,256]{1,0:T(8,128)(2,1)}), bf16[128,256]{1,0:T(8,128)(2,1)}) %reduce-scatter.69.cloned.1.call-update) | async-done | bytes 65552
  1541.5 134.2 %reduce-scatter.77.cloned.1.call-done = f32[32,4]{1,0:T(8,128)} async-done(((f32[1024,4]{1,0:T(8,128)}), f32[32,4]{1,0:T(8,128)}) %reduce-scatter.77.cloned.1.call-update) | async-done | bytes 528
  1677.1 132.3 %reduce-scatter.79.cloned.1.call-done = f32[32,8]{1,0:T(8,128)} async-done(((f32[1024,8]{1,0:T(8,128)}), f32[32,8]{1,0:T(8,128)}) %reduce-scatter.79.cloned.1.call-update) | async-done | bytes 1040
  1810.9 63.4 %reduce-scatter.61.cloned.1.call-done = bf16[128,768]{1,0:T(8,128)(2,1)} async-done(((bf16[1024,768]{1,0:T(8,128)(2,1)}), bf16[128,768]{1,0:T(8,128)(2,1)}) %reduce-scatter.61.cloned.1.call-update) | async-done | bytes 196624
  (312 shorter events, 154.0 us)
Async XLA Ops:
  7.2 239.9 %all-gather.27.cloned.1.call-start = ((), (), s32[]{:S(2)}) async-start(), calls=%async_computation.20 | async-start | bytes 1310720 | tf_op jit(solution)/shard_map/all_gather | solution.py:98
  54.2 27.2 %copy-start.32 = (f32[2,2,32]{2,1,0:T(2,128)S(1)}, f32[2,2,32]{2,1,0:T(2,128)}, u32[]{:S(2)}) copy-start(f32[2,2,32]{2,1,0:T(2,128)} %param.20) | copy-start | bytes 1540
  81.4 66.2 %copy-start.4 = (bf16[128,1024]{1,0:T(8,128)(2,1)S(1)}, bf16[128,1024]{1,0:T(8,128)(2,1)}, u32[]{:S(2)}) copy-start(bf16[128,1024]{1,0:T(8,128)(2,1)} %param.11) | copy-start | bytes 786436
  81.5 67.5 %copy-start.20 = (bf16[2,3,128,256]{3,2,1,0:T(8,128)(2,1)S(1)}, bf16[2,3,128,256]{3,2,1,0:T(8,128)(2,1)}, u32[]{:S(2)}) copy-start(bf16[2,3,128,256]{3,2,1,0:T(8,128)(2,1)} %param.14) | copy-start | bytes 1179652
  121.6 28.4 %copy-start.34 = (bf16[2,2,32]{2,1,0:T(2,128)(2,1)S(1)}, bf16[2,2,32]{2,1,0:T(2,128)(2,1)}, u32[]{:S(2)}) copy-start(bf16[2,2,32]{2,1,0:T(2,128)(2,1)} %param.15) | copy-start | bytes 772
  121.6 28.7 %copy-start.39 = (s32[1,8]{1,0:T(1,128)S(1)}, s32[1,8]{1,0:T(1,128)}, u32[]{:S(2)}) copy-start(s32[1,8]{1,0:T(1,128)} %param.13) | copy-start | bytes 100
  147.6 72.2 %copy-start.31 = (bf16[2,256,128]{2,1,0:T(8,128)(2,1)S(1)}, bf16[2,256,128]{2,1,0:T(8,128)(2,1)}, u32[]{:S(2)}) copy-start(bf16[2,256,128]{2,1,0:T(8,128)(2,1)} %param.16) | copy-start | bytes 393220
  149.0 98.1 %all-gather.43.cloned.1.call-start = ((), (), s32[]{:S(2)}) async-start(), calls=%async_computation.38 | async-start | bytes 1769472 | tf_op jit(solution)/shard_map/all_gather | solution.py:159
  149.9 134.6 %reduce-scatter.41.cloned.1.call-start = ((), (), s32[]{:S(2)}) async-start(), calls=%async_computation.21 | async-start | bytes 2621440 | tf_op jit(solution)/shard_map/reduce_scatter | solution.py:106
  246.9 7.2 copy-start.7
  255.9 30.9 %copy-start.19 = (bf16[2,1024,128]{2,1,0:T(8,128)(2,1)S(1)}, bf16[2,1024,128]{2,1,0:T(8,128)(2,1)}, u32[]{:S(2)}) copy-start(bf16[2,1024,128]{2,1,0:T(8,128)(2,1)} %param.19) | copy-start | bytes 1572868
  255.9 80.4 %all-gather.45.cloned.1.call-start = ((), (), s32[]{:S(2)}) async-start(), calls=%async_computation.39 | async-start | bytes 2359296 | tf_op jit(solution)/shard_map/all_gather | solution.py:161
  256.8 96.7 %all-gather.29.cloned.1.call-start = ((), (), s32[]{:S(2)}) async-start(), calls=%async_computation.22 | async-start | bytes 1310720 | tf_op jit(solution)/shard_map/all_gather | solution.py:98
  286.8 119.6 %all-gather.47.cloned.1.call-start = ((), (), s32[]{:S(2)}) async-start(), calls=%async_computation.40 | async-start | bytes 2359296 | tf_op jit(solution)/shard_map/all_gather | solution.py:162
  287.7 153.3 %reduce-scatter.43.cloned.1.call-start = ((), (), s32[]{:S(2)}) async-start(), calls=%async_computation.23 | async-start | bytes 2621440 | tf_op jit(solution)/shard_map/reduce_scatter | solution.py:106
  411.5 80.9 %all-gather.49.cloned.1.call-start = ((), (), s32[]{:S(2)}) async-start(), calls=%async_computation.41 | async-start | bytes 1769472 | tf_op jit(solution)/shard_map/all_gather | solution.py:159
  412.6 96.8 %all-gather.31.cloned.1.call-start = ((), (), s32[]{:S(2)}) async-start(), calls=%async_computation.24 | async-start | bytes 1310720 | tf_op jit(solution)/shard_map/all_gather | solution.py:98
  443.3 106.2 %reduce-scatter.45.cloned.1.call-start = ((), (), s32[]{:S(2)}) async-start(), calls=%async_computation.25 | async-start | bytes 2621440 | tf_op jit(solution)/shard_map/reduce_scatter | solution.py:106
  472.7 43.7 %copy-start.9 = (bf16[1,256,1024]{2,1,0:T(8,128)(2,1)}, bf16[1,256,1024]{2,1,0:T(8,128)(2,1)S(1)}, u32[]{:S(2)}) copy-start(bf16[1,256,1024]{2,1,0:T(8,128)(2,1)S(1)} %all-gather.8) | copy-start | bytes 1572868
  518.2 83.2 %all-gather.51.cloned.1.call-start = ((), (), s32[]{:S(2)}) async-start(), calls=%async_computation.42 | async-start | bytes 2359296 | tf_op jit(solution)/shard_map/all_gather | solution.py:161
  519.0 99.8 %all-gather.33.cloned.1.call-start = ((), (), s32[]{:S(2)}) async-start(), calls=%async_computation.26 | async-start | bytes 1310720 | tf_op jit(solution)/shard_map/all_gather | solution.py:98
  551.9 85.2 %all-gather.35.cloned.1.call-start = ((), (), s32[]{:S(2)}) async-start(), calls=%async_computation.28 | async-start | bytes 1310720 | tf_op jit(solution)/shard_map/all_gather | solution.py:102
  552.6 137.3 %all-gather.53.cloned.1.call-start = ((), (), s32[]{:S(2)}) async-start(), calls=%async_computation.43 | async-start | bytes 2359296 | tf_op jit(solution)/shard_map/all_gather | solution.py:162
  553.2 168.3 %reduce-scatter.49.cloned.1.call-start = ((), (), s32[]{:S(2)}) async-start(), calls=%async_computation.29 | async-start | bytes 1310720 | tf_op jit(solution)/shard_map/reduce_scatter | solution.py:115
  698.3 56.7 %reduce-scatter.47.cloned.1.call-start = ((), (), s32[]{:S(2)}) async-start(), calls=%async_computation.27 | async-start | bytes 2621440 | tf_op jit(solution)/shard_map/reduce_scatter | solution.py:106
  703.5 71.3 %all-gather.37.cloned.1.call-start = ((), (), s32[]{:S(2)}) async-start(), calls=%async_computation.30 | async-start | bytes 1310720 | tf_op jit(solution)/shard_map/all_gather | solution.py:102
  757.2 19.6 %copy-start.30 = (bf16[1,512,256]{1,2,0:T(8,128)(2,1)S(1)}, bf16[1,512,256]{1,2,0:T(8,128)(2,1)}, u32[]{:S(2)}) copy-start(bf16[1,512,256]{1,2,0:T(8,128)(2,1)} %copy-done.29) | copy-start | bytes 786436
  757.9 56.6 %reduce-scatter.51.cloned.1.call-start = ((), (), s32[]{:S(2)}) async-start(), calls=%async_computation.31 | async-start | bytes 1310720 | tf_op jit(solution)/shard_map/reduce_scatter | solution.py:115
  789.6 45.0 %all-gather.39.cloned.1.call-start = ((), (), s32[]{:S(2)}) async-start(), calls=%async_computation.32 | async-start | bytes 1310720 | tf_op jit(solution)/shard_map/all_gather | solution.py:102
  817.7 50.3 %reduce-scatter.53.cloned.1.call-start = ((), (), s32[]{:S(2)}) async-start(), calls=%async_computation.33 | async-start | bytes 1310720 | tf_op jit(solution)/shard_map/reduce_scatter | solution.py:115
  843.1 45.0 %copy-start.8 = (bf16[1,256,1024]{2,1,0:T(8,128)(2,1)S(1)}, bf16[1,256,1024]{2,1,0:T(8,128)(2,1)}, u32[]{:S(2)}) copy-start(bf16[1,256,1024]{2,1,0:T(8,128)(2,1)} %copy-done.7) | copy-start | bytes 1572868
  843.1 45.0 %copy-start.14 = (bf16[4,64,512]{2,1,0:T(8,128)(2,1)S(1)}, bf16[4,64,512]{2,1,0:T(8,128)(2,1)}, u32[]{:S(2)}) copy-start(bf16[4,64,512]{2,1,0:T(8,128)(2,1)} %copy-done.13) | copy-start | bytes 786436
  843.1 45.0 %all-gather.41.cloned.1.call-start = ((), (), s32[]{:S(2)}) async-start(), calls=%async_computation.34 | async-start | bytes 1310720 | tf_op jit(solution)/shard_map/all_gather | solution.py:102
  870.5 19.4 %copy-start.28 = (bf16[1,512,256]{1,2,0:T(8,128)(2,1)S(1)}, bf16[1,512,256]{1,2,0:T(8,128)(2,1)}, u32[]{:S(2)}) copy-start(bf16[1,512,256]{1,2,0:T(8,128)(2,1)} %copy-done.27) | copy-start | bytes 786436
  871.2 65.2 %reduce-scatter.55.cloned.1.call-start = ((), (), s32[]{:S(2)}) async-start(), calls=%async_computation.35 | async-start | bytes 1310720 | tf_op jit(solution)/shard_map/reduce_scatter | solution.py:115
  900.9 97.3 %reduce-scatter.75.cloned.1.call-start = ((), (), s32[]{:S(2)}) async-start(), calls=%async_computation.51 | async-start | bytes 2359296
  907.1 155.9 %reduce-scatter.67.cloned.1.call-start = ((), (), s32[]{:S(2)}) async-start(), calls=%async_computation.47 | async-start | bytes 73728
  908.1 220.5 %reduce-scatter.71.cloned.1.call-start = ((), (), s32[]{:S(2)}) async-start(), calls=%async_computation.49 | async-start | bytes 589824
  909.9 286.4 %reduce-scatter.63.cloned.1.call-start = ((), (), s32[]{:S(2)}) async-start(), calls=%async_computation.45 | async-start | bytes 1769472
  918.0 342.9 %reduce-scatter.65.cloned.1.call-start = ((), (), s32[]{:S(2)}) async-start(), calls=%async_computation.46 | async-start | bytes 73728
  919.0 412.8 %reduce-scatter.73.cloned.1.call-start = ((), (), s32[]{:S(2)}) async-start(), calls=%async_computation.50 | async-start | bytes 2359296
  925.2 477.5 %reduce-scatter.59.cloned.1.call-start = ((), (), s32[]{:S(2)}) async-start(), calls=%async_computation.37 | async-start | bytes 2359296 | tf_op jit(solution)/shard_map/reduce_scatter | solution.py:276
  929.4 543.7 %reduce-scatter.57.cloned.1.call-start = ((), (), s32[]{:S(2)}) async-start(), calls=%async_computation.36 | async-start | bytes 2359296 | tf_op jit(solution)/shard_map/reduce_scatter | solution.py:276
  933.6 605.2 %reduce-scatter.69.cloned.1.call-start = ((), (), s32[]{:S(2)}) async-start(), calls=%async_computation.48 | async-start | bytes 589824
  936.3 739.4 %reduce-scatter.77.cloned.1.call-start = ((), (), s32[]{:S(2)}) async-start(), calls=%async_computation.52 | async-start | bytes 540672
  939.7 869.8 %reduce-scatter.79.cloned.1.call-start = ((), (), s32[]{:S(2)}) async-start(), calls=%async_computation.53 | async-start | bytes 540672
  941.8 932.5 %reduce-scatter.61.cloned.1.call-start = ((), (), s32[]{:S(2)}) async-start(), calls=%async_computation.44 | async-start | bytes 1769472
  1331.8 208.7 %copy-start.12 = (bf16[128,1024]{1,0:T(8,128)(2,1)S(1)}, bf16[128,1024]{1,0:T(8,128)(2,1)}, u32[]{:S(2)}) copy-start(bf16[128,1024]{1,0:T(8,128)(2,1)} %reduce-scatter.55.cloned.1.call-done) | copy-start | bytes 786436
  (31 other events, 73.7 us)
Sparse Core Ops, SparseCore 0:
  149.1 14.1 all-gather.26
  165.9 45.5 all-gather.42
  256.0 28.3 reduce-scatter.40
  287.0 49.2 all-gather.44
  338.3 15.2 all-gather.28
  356.0 50.3 all-gather.46
  411.6 29.3 reduce-scatter.42
  443.6 48.6 all-gather.48
  494.5 14.8 all-gather.30
  518.3 31.1 reduce-scatter.44
  552.3 49.1 all-gather.50
  603.5 15.2 all-gather.32
  620.3 16.6 all-gather.34
  639.5 50.3 all-gather.52
  698.4 22.9 reduce-scatter.48
  723.8 31.1 reduce-scatter.46
  758.1 16.7 all-gather.36
  789.7 24.7 reduce-scatter.50
  817.9 16.7 all-gather.38
  843.2 24.7 reduce-scatter.52
  871.3 16.6 all-gather.40
  901.0 24.8 reduce-scatter.54
  929.4 68.7 reduce-scatter.74
  1001.5 61.4 reduce-scatter.66
  1066.9 61.5 reduce-scatter.70
  1131.8 64.4 reduce-scatter.62
  1199.6 61.3 reduce-scatter.64
  1264.4 67.2 reduce-scatter.72
  1335.3 67.3 reduce-scatter.58
  1406.0 67.0 reduce-scatter.56
  1477.0 61.6 reduce-scatter.68
  1541.0 134.6 reduce-scatter.76
  1677.7 131.6 reduce-scatter.78
  1812.9 61.3 reduce-scatter.60
where the time goes:
time: 1890 us; the launch traced here: 1880 us
  waiting for transfers between devices  1370 us (72%)
  blocking collectives  265 us (14%)
  local copies, waits for them, and re-layouts  105 us (6%)
  matrix products  91.5 us (5%)
  other arithmetic  35.7 us (2%)
    unnamed x44, waiting for transfers between devices  751 us
    reduce_scatter x2, waiting for transfers between devices, body(): lax.psum_scatter(layer_grads[3].astype(jnp.bfloat16), 'fsdp', scatter_dim...  139 us
    reduce_scatter x4, waiting for transfers between devices, sum_branch(): lax.psum_scatter(partial_fn(jnp.int32(0), tok_rows * lax.axis_size('tp'))...  119 us
    all_gather x2, waiting for transfers between devices, body(): lax.all_gather(proj_weight[layer_id], 'fsdp', axis=1, tiled=True)  101 us
    reduce_scatter x4, waiting for transfers between devices, sum_inputs(): lax.psum_scatter(partial_fn(jnp.int32(0), tok_rows * lax.axis_size('tp'))...  67.3 us
    all_gather x4, waiting for transfers between devices, gather_grads(): return lax.all_gather(values, 'tp', axis=0, tiled=True)  64.1 us
    all_gather x2, blocking collectives, body(): lax.all_gather(qv_bias[layer_id], 'fsdp', axis=1, tiled=True)  62 us
    all_gather x2, blocking collectives, body(): lax.all_gather(out_weight[layer_id], 'fsdp', axis=1, tiled=True)  56.4 us
  transfers between devices with their start and end apart: 34, of which 31 were waited for; matrix products, arithmetic and copies ran while one was open for 5% of the time, Pallas kernels for 0%

commit v1 on v0

--- a/solution.py
+++ b/solution.py
@@ -155,11 +155,26 @@
     residual = inputs.astype(jnp.float32)
     saved_acts = []
     for layer_id in range(LAYERS):
+
+        def perform_teams_all(shard_in, bus_axis):
+            high = lax.axis_index(bus_axis)
+            carry_in = lax.axis_size(bus_axis)
+            carry_out, back, latest = (carry_in, high, shard_in.shape[1])
+            block_out, view_out = (shard_in, 1)
+            while view_out < carry_out:
+                everything = range(carry_out)
+                g_now = list(map(lambda b: (b, (b - view_out) % carry_out), everything))
+                block_out = jnp.concatenate(
+                    [block_out, lax.ppermute(block_out, bus_axis, g_now)], axis=1
+                )
+                view_out = 2 * view_out
+            return jnp.roll(block_out, back * latest, axis=1)
+
         weights = (
             lax.all_gather(qkv_weight[layer_id], "fsdp", axis=1, tiled=True),
             lax.all_gather(out_weight[layer_id], "fsdp", axis=1, tiled=True),
             lax.all_gather(fc_weight[layer_id], "fsdp", axis=0, tiled=True),
-            lax.all_gather(proj_weight[layer_id], "fsdp", axis=1, tiled=True),
+            perform_teams_all(proj_weight[layer_id], "fsdp"),
             lax.all_gather(qv_bias[layer_id], "fsdp", axis=1, tiled=True),
             lax.all_gather(fc_bias[layer_id], "fsdp", axis=0, tiled=True),
         )

time: 1890 us -> 1970 us (1.042)
  waiting for transfers between devices: 1370 us -> 1410 us
  blocking collectives: 265 us -> 286 us
    ppermute x0 -> x6, waiting for transfers between devices: none -> 64.6 us  [perform_teams_all(): lax.ppermute(block_out, bus_axis, g_now)]
    unnamed x126 -> x134, local copies, waits for them, and re-layouts: 47.3 us -> 48.4 us
  transfers between devices with their start and end apart: 34 -> 40, of which waited for: 31 -> 32; matrix products, arithmetic and copies ran while one was open for 5% -> 5% of each run, Pallas kernels for 0% -> 0%
where the time goes in v1:
time: 1970 us; the launch traced here: 1960 us
  waiting for transfers between devices  1410 us (72%)
  blocking collectives  286 us (15%)
  local copies, waits for them, and re-layouts  107 us (5%)
  matrix products  94.2 us (5%)
  other arithmetic  37.9 us (2%)
    unnamed x44, waiting for transfers between devices  752 us
    reduce_scatter x2, waiting for transfers between devices, body(): lax.psum_scatter(layer_grads[3].astype(jnp.bfloat16), 'fsdp', scatter_dim...  140 us
    reduce_scatter x4, waiting for transfers between devices, sum_branch(): lax.psum_scatter(partial_fn(jnp.int32(0), tok_rows * lax.axis_size('tp'))...  118 us
    all_gather x2, waiting for transfers between devices, body(): lax.all_gather(proj_weight[layer_id], 'fsdp', axis=1, tiled=True)  102 us
    ppermute x6, waiting for transfers between devices, perform_teams_all(): lax.ppermute(block_out, bus_axis, g_now)  64.6 us
    all_gather x4, waiting for transfers between devices, gather_grads(): return lax.all_gather(values, 'tp', axis=0, tiled=True)  63.9 us
    all_gather x2, blocking collectives, body(): lax.all_gather(qv_bias[layer_id], 'fsdp', axis=1, tiled=True)  62 us
    all_gather x2, blocking collectives, body(): lax.all_gather(fc_bias[layer_id], 'fsdp', axis=0, tiled=True)  60.4 us
  transfers between devices with their start and end apart: 40, of which 32 were waited for; matrix products, arithmetic and copies ran while one was open for 5% of the time, Pallas kernels for 0%

profile of v1, /device:TPU:0, one launch (start us, length us, event | category | flops | bytes accessed | tf_op | source)
XLA Modules:
  0.0 1963.6 jit_solution(6432219855208353484)
XLA Ops:
  8.0 46.2 %all_gather.73 = f32[2,4,1024]{1,0,2:T(2,128)S(1)} all-gather(f32[2,4,32]{1,0,2:T(2,128)S(1)} %copy.99), channel_id=1, replica_groups=mesh['fsdp'=8,'tp'=4] {'fsdp','tp'}, dimensions={2}, use_global_device_ids=true | all-gather | bytes 33792 | tf_op jit(solution)/shard_map/all_gather | solution.py:152
  54.2 27.3 %slice_reduce_fusion = (f32[1024]{0:T(1024)S(1)}, f32[1024]{0:T(1024)S(1)}, f32[1024]{0:T(1024)S(1)}, f32[1024]{0:T(1024)S(1)}, f32[1024]{0:T(1024)S(1)}, /*inde...) fusion(f32[2,4,1024]{1,0,2:T(2,128)S(1)} %all_gather.73), kind=kLoop, calls=%fused_computation.178 | loop fusion | bytes 65536 | tf_op jit(solution)/shard_map/slice | solution.py:214
  81.7 40.2 %all_gather.72 = f32[2,2,1024]{1,0,2:T(2,128)S(1)} all-gather(f32[2,2,32]{1,0,2:T(2,128)S(1)} %copy.98), channel_id=1, replica_groups=mesh['fsdp'=8,'tp'=4] {'fsdp','tp'}, dimensions={2}, use_global_device_ids=true | all-gather | bytes 16896 | tf_op jit(solution)/shard_map/all_gather | solution.py:151
  121.8 26.0 %slice_reduce_fusion.2 = (f32[1024]{0:T(1024)S(1)}, f32[1024]{0:T(1024)S(1)}, f32[1024]{0:T(1024)S(1)}, f32[1024]{0:T(1024)S(1)}) fusion(f32[2,2,1024]{1,0,2:T(2,128)S(1)} %all_gather.72), kind=kLoop, calls=%fused_computation.180 | loop fusion | bytes 32768 | tf_op jit(solution)/shard_map/slice | solution.py:205
  151.4 30.6 %all-gather.6 = bf16[1,2,256]{1,0,2:T(2,128)(2,1)S(1)} all-gather(bf16[1,2,32]{1,0,2:T(2,128)(2,1)S(1)} %copy.162), channel_id=8, replica_groups=mesh['fsdp'=8,'tp'=4] {'fsdp'}, dimensions={2}, use_global_device_ids=true | all-gather | bytes 1152 | tf_op jit(solution)/shard_map/all_gather | solution.py:178
  182.0 31.4 %all-gather.1 = bf16[1,2,256]{1,0,2:T(2,128)(2,1)S(1)} all-gather(bf16[1,2,32]{1,0,2:T(2,128)(2,1)S(1)} %copy.160), channel_id=3, replica_groups=mesh['fsdp'=8,'tp'=4] {'fsdp'}, dimensions={2}, use_global_device_ids=true | all-gather | bytes 1152 | tf_op jit(solution)/shard_map/all_gather | solution.py:178
  220.8 27.1 %all-gather.2 = bf16[1,256,1024]{2,1,0:T(8,128)(2,1)S(1)} all-gather(bf16[1,256,128]{2,1,0:T(8,128)(2,1)S(1)} %get-tuple-element.122), channel_id=4, replica_groups=mesh['fsdp'=8,'tp'=4] {'fsdp'}, dimensions={2}, use_global_device_ids=true | all-gather | bytes 589824 | tf_op jit(solution)/shard_map/all_gather | solution.py:175
  258.9 28.9 %reduce-scatter.41.cloned.1.call-done = f32[128,1024]{1,0:T(8,128)} async-done(((f32[512,1024]{1,0:T(8,128)}), f32[128,1024]{1,0:T(8,128)}) %reduce-scatter.41.cloned.1.call-update) | async-done | bytes 524304 | tf_op jit(solution)/shard_map/reduce_scatter | solution.py:106
  293.7 19.0 collective-permute-done.1
  313.4 37.0 %all-gather.4 = bf16[1,1024]{1,0:T(2,128)(2,1)S(1)} all-gather(bf16[1,128]{1,0:T(2,128)(2,1)S(1)} %get-tuple-element.126), channel_id=6, replica_groups=mesh['fsdp'=8,'tp'=4] {'fsdp'}, dimensions={1}, use_global_device_ids=true | all-gather | bytes 2304 | tf_op jit(solution)/shard_map/all_gather | solution.py:179
  350.4 21.9 %all-gather.45.cloned.1.call-done = bf16[1,1024,1024]{2,1,0:T(8,128)(2,1)} async-done(((bf16[1,128,1024]{2,1,0:T(8,128)(2,1)}), bf16[1,1024,1024]{2,1,0:T(8,128)(2,1)}) %all-gather.45.cloned.1.call-update) | async-done | bytes 2097168 | tf_op jit(solution)/shard_map/all_gather | solution.py:176
  372.3 22.5 %all-gather.29.cloned.1.call-done = bf16[512,1024]{1,0:T(8,128)(2,1)} async-done(((bf16[128,1024]{1,0:T(8,128)(2,1)}), bf16[512,1024]{1,0:T(8,128)(2,1)}) %all-gather.29.cloned.1.call-update) | async-done | bytes 1048592 | tf_op jit(solution)/shard_map/all_gather | solution.py:98
  399.4 6.9 fusion.42
  408.1 29.5 %reduce-scatter.43.cloned.1.call-done = f32[128,1024]{1,0:T(8,128)} async-done(((f32[512,1024]{1,0:T(8,128)}), f32[128,1024]{1,0:T(8,128)}) %reduce-scatter.43.cloned.1.call-update) | async-done | bytes 524304 | tf_op jit(solution)/shard_map/reduce_scatter | solution.py:106
  440.0 31.1 %all-gather.7 = bf16[1,256,1024]{2,1,0:T(8,128)(2,1)} all-gather(bf16[1,256,128]{2,1,0:T(8,128)(2,1)S(1)} %get-tuple-element.121), channel_id=9, replica_groups=mesh['fsdp'=8,'tp'=4] {'fsdp'}, dimensions={2}, use_global_device_ids=true | all-gather | bytes 589824 | tf_op jit(solution)/shard_map/all_gather | solution.py:175
  471.1 16.2 all-gather.47.cloned.1.call-done
  487.3 17.0 all-gather.31.cloned.1.call-done
  513.8 30.7 %reduce-scatter.45.cloned.1.call-done = f32[128,1024]{1,0:T(8,128)} async-done(((f32[512,1024]{1,0:T(8,128)}), f32[128,1024]{1,0:T(8,128)}) %reduce-scatter.45.cloned.1.call-update) | async-done | bytes 524304 | tf_op jit(solution)/shard_map/reduce_scatter | solution.py:106
  552.5 23.4 %all-gather.9 = bf16[1,1024]{1,0:T(2,128)(2,1)S(1)} all-gather(bf16[1,128]{1,0:T(2,128)(2,1)S(1)} %get-tuple-element.125), channel_id=11, replica_groups=mesh['fsdp'=8,'tp'=4] {'fsdp'}, dimensions={1}, use_global_device_ids=true | all-gather | bytes 2304 | tf_op jit(solution)/shard_map/all_gather | solution.py:179
  577.2 22.9 %all-gather.49.cloned.1.call-done = bf16[1,1024,1024]{2,1,0:T(8,128)(2,1)} async-done(((bf16[1,128,1024]{2,1,0:T(8,128)(2,1)}), bf16[1,1024,1024]{2,1,0:T(8,128)(2,1)}) %all-gather.49.cloned.1.call-update) | async-done | bytes 2097168 | tf_op jit(solution)/shard_map/all_gather | solution.py:176
  600.1 19.0 all-gather.33.cloned.1.call-done
  619.1 4.5 fusion.36
  623.7 13.6 all-gather.35.cloned.1.call-done
  637.3 53.0 %all-gather.51.cloned.1.call-done = bf16[1,1024,1024]{2,1,0:T(8,128)(2,1)} async-done(((bf16[1,1024,128]{2,1,0:T(8,128)(2,1)}), bf16[1,1024,1024]{2,1,0:T(8,128)(2,1)}) %all-gather.51.cloned.1.call-update) | async-done | bytes 2097168 | tf_op jit(solution)/shard_map/all_gather | solution.py:229
  690.3 5.2 fusion.169
  701.7 45.6 %collective-permute-done.5 = bf16[1024,512]{1,0:T(8,128)(2,1)S(1)} collective-permute-done((bf16[1024,512]{1,0:T(8,128)(2,1)S(1)}, bf16[1024,512]{1,0:T(8,128)(2,1)S(1)}, u32[]{:S(2)}, u32[]{:S(2)}) %collective-permute-start.5) | collective-permute-done | bytes 1048608 | tf_op jit(solution)/shard_map/ppermute | solution.py:168
  747.3 6.7 fusion.44
  755.4 29.3 %reduce-scatter.47.cloned.1.call-done = f32[128,1024]{1,0:T(8,128)} async-done(((f32[512,1024]{1,0:T(8,128)}), f32[128,1024]{1,0:T(8,128)}) %reduce-scatter.47.cloned.1.call-update) | async-done | bytes 524304 | tf_op jit(solution)/shard_map/reduce_scatter | solution.py:106
  787.8 16.6 all-gather.37.cloned.1.call-done
  819.8 24.3 %reduce-scatter.51.cloned.1.call-done = bf16[128,1024]{1,0:T(8,128)(2,1)} async-done(((bf16[512,1024]{1,0:T(8,128)(2,1)}), bf16[128,1024]{1,0:T(8,128)(2,1)}) %reduce-scatter.51.cloned.1.call-update) | async-done | bytes 262160 | tf_op jit(solution)/shard_map/reduce_scatter | solution.py:115
  847.4 49.0 %all-gather.53.cloned.1.call-done = bf16[1,1024,1024]{2,1,0:T(8,128)(2,1)} async-done(((bf16[1,1024,128]{2,1,0:T(8,128)(2,1)}), bf16[1,1024,1024]{2,1,0:T(8,128)(2,1)}) %all-gather.53.cloned.1.call-update) | async-done | bytes 2097168 | tf_op jit(solution)/shard_map/all_gather | solution.py:229
  896.4 17.0 all-gather.39.cloned.1.call-done
  913.4 5.2 fusion.170
  921.9 24.9 %reduce-scatter.53.cloned.1.call-done = bf16[128,1024]{1,0:T(8,128)(2,1)} async-done(((bf16[512,1024]{1,0:T(8,128)(2,1)}), bf16[128,1024]{1,0:T(8,128)(2,1)}) %reduce-scatter.53.cloned.1.call-update) | async-done | bytes 262160 | tf_op jit(solution)/shard_map/reduce_scatter | solution.py:115
  950.3 16.6 all-gather.41.cloned.1.call-done
  1029.3 47.3 %reduce-scatter.75.cloned.1.call-done = bf16[128,1024]{1,0:T(8,128)(2,1)} async-done(((bf16[1024,1024]{1,0:T(8,128)(2,1)}), bf16[128,1024]{1,0:T(8,128)(2,1)}) %reduce-scatter.75.cloned.1.call-update) | async-done | bytes 262160
  1077.8 63.6 %reduce-scatter.67.cloned.1.call-done = bf16[32,2]{1,0:T(8,128)(2,1)} async-done(((bf16[256,2]{1,0:T(8,128)(2,1)}), bf16[32,2]{1,0:T(8,128)(2,1)}) %reduce-scatter.67.cloned.1.call-update) | async-done | bytes 144
  1142.2 64.9 %reduce-scatter.71.cloned.1.call-done = bf16[128,256]{1,0:T(8,128)(2,1)} async-done(((bf16[1024,256]{1,0:T(8,128)(2,1)}), bf16[128,256]{1,0:T(8,128)(2,1)}) %reduce-scatter.71.cloned.1.call-update) | async-done | bytes 65552
  1208.0 66.9 %reduce-scatter.63.cloned.1.call-done = bf16[128,768]{1,0:T(8,128)(2,1)} async-done(((bf16[1024,768]{1,0:T(8,128)(2,1)}), bf16[128,768]{1,0:T(8,128)(2,1)}) %reduce-scatter.63.cloned.1.call-update) | async-done | bytes 196624
  1276.1 19.2 all-reduce.2
  1296.0 44.0 %reduce-scatter.65.cloned.1.call-done = bf16[32,2]{1,0:T(8,128)(2,1)} async-done(((bf16[256,2]{1,0:T(8,128)(2,1)}), bf16[32,2]{1,0:T(8,128)(2,1)}) %reduce-scatter.65.cloned.1.call-update) | async-done | bytes 144
  1341.4 69.5 %reduce-scatter.73.cloned.1.call-done = bf16[128,1024]{1,0:T(8,128)(2,1)} async-done(((bf16[1024,1024]{1,0:T(8,128)(2,1)}), bf16[128,1024]{1,0:T(8,128)(2,1)}) %reduce-scatter.73.cloned.1.call-update) | async-done | bytes 262160
  1412.0 69.7 %reduce-scatter.59.cloned.1.call-done = bf16[128,1024]{1,0:T(8,128)(2,1)} async-done(((bf16[1024,1024]{1,0:T(8,128)(2,1)}), bf16[128,1024]{1,0:T(8,128)(2,1)}) %reduce-scatter.59.cloned.1.call-update) | async-done | bytes 262160 | tf_op jit(solution)/shard_map/reduce_scatter | solution.py:291
  1481.7 70.7 %reduce-scatter.57.cloned.1.call-done = bf16[128,1024]{1,0:T(8,128)(2,1)} async-done(((bf16[1024,1024]{1,0:T(8,128)(2,1)}), bf16[128,1024]{1,0:T(8,128)(2,1)}) %reduce-scatter.57.cloned.1.call-update) | async-done | bytes 262160 | tf_op jit(solution)/shard_map/reduce_scatter | solution.py:291
  1555.5 62.6 %reduce-scatter.69.cloned.1.call-done = bf16[128,256]{1,0:T(8,128)(2,1)} async-done(((bf16[1024,256]{1,0:T(8,128)(2,1)}), bf16[128,256]{1,0:T(8,128)(2,1)}) %reduce-scatter.69.cloned.1.call-update) | async-done | bytes 65552
  1620.8 134.2 %reduce-scatter.77.cloned.1.call-done = f32[32,4]{1,0:T(8,128)} async-done(((f32[1024,4]{1,0:T(8,128)}), f32[32,4]{1,0:T(8,128)}) %reduce-scatter.77.cloned.1.call-update) | async-done | bytes 528
  1756.5 132.4 %reduce-scatter.79.cloned.1.call-done = f32[32,8]{1,0:T(8,128)} async-done(((f32[1024,8]{1,0:T(8,128)}), f32[32,8]{1,0:T(8,128)}) %reduce-scatter.79.cloned.1.call-update) | async-done | bytes 1040
  1890.4 63.6 %reduce-scatter.61.cloned.1.call-done = bf16[128,768]{1,0:T(8,128)(2,1)} async-done(((bf16[1024,768]{1,0:T(8,128)(2,1)}), bf16[128,768]{1,0:T(8,128)(2,1)}) %reduce-scatter.61.cloned.1.call-update) | async-done | bytes 196624
  (336 shorter events, 172.1 us)
Async XLA Ops:
  7.2 241.0 %all-gather.27.cloned.1.call-start = ((), (), s32[]{:S(2)}) async-start(), calls=%async_computation.20 | async-start | bytes 1310720 | tf_op jit(solution)/shard_map/all_gather | solution.py:98
  81.6 66.3 %copy-start.4 = (bf16[128,1024]{1,0:T(8,128)(2,1)S(1)}, bf16[128,1024]{1,0:T(8,128)(2,1)}, u32[]{:S(2)}) copy-start(bf16[128,1024]{1,0:T(8,128)(2,1)} %param.13) | copy-start | bytes 786436
  81.7 67.6 %copy-start.23 = (bf16[2,3,128,256]{3,2,1,0:T(8,128)(2,1)S(1)}, bf16[2,3,128,256]{3,2,1,0:T(8,128)(2,1)}, u32[]{:S(2)}) copy-start(bf16[2,3,128,256]{3,2,1,0:T(8,128)(2,1)} %param.16) | copy-start | bytes 1179652
  121.8 29.3 %copy-start.41 = (s32[1,8]{1,0:T(1,128)S(1)}, s32[1,8]{1,0:T(1,128)}, u32[]{:S(2)}) copy-start(s32[1,8]{1,0:T(1,128)} %param.15) | copy-start | bytes 100
  147.9 72.9 %copy-start.33 = (bf16[2,256,128]{2,1,0:T(8,128)(2,1)S(1)}, bf16[2,256,128]{2,1,0:T(8,128)(2,1)}, u32[]{:S(2)}) copy-start(bf16[2,256,128]{2,1,0:T(8,128)(2,1)} %param.18) | copy-start | bytes 393220
  149.2 99.0 %all-gather.43.cloned.1.call-start = ((), (), s32[]{:S(2)}) async-start(), calls=%async_computation.38 | async-start | bytes 1769472 | tf_op jit(solution)/shard_map/all_gather | solution.py:174
  150.8 137.0 %reduce-scatter.41.cloned.1.call-start = ((), (), s32[]{:S(2)}) async-start(), calls=%async_computation.21 | async-start | bytes 2621440 | tf_op jit(solution)/shard_map/reduce_scatter | solution.py:106
  257.0 115.3 %all-gather.45.cloned.1.call-start = ((), (), s32[]{:S(2)}) async-start(), calls=%async_computation.39 | async-start | bytes 2359296 | tf_op jit(solution)/shard_map/all_gather | solution.py:176
  257.9 136.8 %all-gather.29.cloned.1.call-start = ((), (), s32[]{:S(2)}) async-start(), calls=%async_computation.22 | async-start | bytes 1310720 | tf_op jit(solution)/shard_map/all_gather | solution.py:98
  258.9 31.3 %collective-permute-start = (bf16[1024,128]{1,0:T(8,128)(2,1)S(1)}, bf16[1024,128]{1,0:T(8,128)(2,1)S(1)}, u32[]{:S(2)}, u32[]{:S(2)}) collective-permute-start(bf16[1024,128]{1,0:T(8,128)(2,1)S(1)} %get-tuple-element.112), channel_id=1, source_target_pairs={{0,28},{4,0},{8,4},{12,8},{16,12},{20,16},{24,20},{28,24},{1,29},{... | collective-permute-start | bytes 786440 | tf_op jit(solution)/shard_map/ppermute | solution.py:168
  290.2 147.5 %reduce-scatter.43.cloned.1.call-start = ((), (), s32[]{:S(2)}) async-start(), calls=%async_computation.23 | async-start | bytes 2621440 | tf_op jit(solution)/shard_map/reduce_scatter | solution.py:106
  290.3 22.3 %collective-permute-start.1 = (bf16[1024,256]{1,0:T(8,128)(2,1)S(1)}, bf16[1024,256]{1,0:T(8,128)(2,1)S(1)}, u32[]{:S(2)}, u32[]{:S(2)}) collective-permute-start(bf16[1024,256]{1,0:T(8,128)(2,1)S(1)} %pad_maximum_fusion.4), channel_id=1, source_target_pairs={{0,24},{4,28},{8,0},{12,4},{16,8},{20,12},{24,16},{28,20},{1,25},{... | collective-permute-start | bytes 1572872 | tf_op jit(solution)/shard_map/ppermute | solution.py:168
  312.7 85.2 %collective-permute-start.2 = (bf16[1024,512]{1,0:T(8,128)(2,1)S(1)}, bf16[1024,512]{1,0:T(8,128)(2,1)}, u32[]{:S(2)}, u32[]{:S(2)}) collective-permute-start(bf16[1024,512]{1,0:T(8,128)(2,1)S(1)} %pad_maximum_fusion), channel_id=1, source_target_pairs={{0,16},{4,20},{8,24},{12,28},{16,0},{20,4},{24,8},{28,12},{1,17},{... | collective-permute-start | bytes 3145736 | tf_op jit(solution)/shard_map/ppermute | solution.py:168
  406.3 81.0 %all-gather.47.cloned.1.call-start = ((), (), s32[]{:S(2)}) async-start(), calls=%async_computation.40 | async-start | bytes 1769472 | tf_op jit(solution)/shard_map/all_gather | solution.py:174
  408.0 96.3 %all-gather.31.cloned.1.call-start = ((), (), s32[]{:S(2)}) async-start(), calls=%async_computation.24 | async-start | bytes 1310720 | tf_op jit(solution)/shard_map/all_gather | solution.py:98
  439.9 104.6 %reduce-scatter.45.cloned.1.call-start = ((), (), s32[]{:S(2)}) async-start(), calls=%async_computation.25 | async-start | bytes 2621440 | tf_op jit(solution)/shard_map/reduce_scatter | solution.py:106
  513.2 86.9 %all-gather.49.cloned.1.call-start = ((), (), s32[]{:S(2)}) async-start(), calls=%async_computation.41 | async-start | bytes 2359296 | tf_op jit(solution)/shard_map/all_gather | solution.py:176
  513.8 105.3 %all-gather.33.cloned.1.call-start = ((), (), s32[]{:S(2)}) async-start(), calls=%async_computation.26 | async-start | bytes 1310720 | tf_op jit(solution)/shard_map/all_gather | solution.py:98
  546.8 90.5 %all-gather.35.cloned.1.call-start = ((), (), s32[]{:S(2)}) async-start(), calls=%async_computation.28 | async-start | bytes 1310720 | tf_op jit(solution)/shard_map/all_gather | solution.py:102
  547.4 142.9 %all-gather.51.cloned.1.call-start = ((), (), s32[]{:S(2)}) async-start(), calls=%async_computation.42 | async-start | bytes 2359296 | tf_op jit(solution)/shard_map/all_gather | solution.py:229
  548.1 206.0 %reduce-scatter.49.cloned.1.call-start = ((), (), s32[]{:S(2)}) async-start(), calls=%async_computation.29 | async-start | bytes 1310720 | tf_op jit(solution)/shard_map/reduce_scatter | solution.py:115
  548.2 27.7 %collective-permute-start.3 = (bf16[1024,128]{1,0:T(8,128)(2,1)S(1)}, bf16[1024,128]{1,0:T(8,128)(2,1)S(1)}, u32[]{:S(2)}, u32[]{:S(2)}) collective-permute-start(bf16[1024,128]{1,0:T(8,128)(2,1)S(1)} %get-tuple-element.113), channel_id=1, source_target_pairs={{0,28},{4,0},{8,4},{12,8},{16,12},{20,16},{24,20},{28,24},{1,29},{... | collective-permute-start | bytes 786440 | tf_op jit(solution)/shard_map/ppermute | solution.py:168
  576.8 122.0 %collective-permute-start.4 = (bf16[1024,256]{1,0:T(8,128)(2,1)}, bf16[1024,256]{1,0:T(8,128)(2,1)}, u32[]{:S(2)}, u32[]{:S(2)}) collective-permute-start(bf16[1024,256]{1,0:T(8,128)(2,1)} %pad_maximum_fusion.5), channel_id=1, source_target_pairs={{0,24},{4,28},{8,0},{12,4},{16,8},{20,12},{24,16},{28,20},{1,25},{... | collective-permute-start | bytes 1572872 | tf_op jit(solution)/shard_map/ppermute | solution.py:168
  698.7 85.9 %reduce-scatter.47.cloned.1.call-start = ((), (), s32[]{:S(2)}) async-start(), calls=%async_computation.27 | async-start | bytes 2621440 | tf_op jit(solution)/shard_map/reduce_scatter | solution.py:106
  698.8 48.5 %copy-start.44 = (f32[512,1024]{1,0:T(8,128)S(1)}, f32[512,1024]{1,0:T(8,128)}, u32[]{:S(2)}) copy-start(f32[512,1024]{1,0:T(8,128)} %fusion.36) | copy-start | bytes 6291460
  700.1 47.2 %collective-permute-start.5 = (bf16[1024,512]{1,0:T(8,128)(2,1)S(1)}, bf16[1024,512]{1,0:T(8,128)(2,1)S(1)}, u32[]{:S(2)}, u32[]{:S(2)}) collective-permute-start(bf16[1024,512]{1,0:T(8,128)(2,1)S(1)} %pad_maximum_fusion.1), channel_id=1, source_target_pairs={{0,16},{4,20},{8,24},{12,28},{16,0},{20,4},{24,8},{28,12},{1,17},{... | collective-permute-start | bytes 3145736 | tf_op jit(solution)/shard_map/ppermute | solution.py:168
  754.0 50.4 %all-gather.37.cloned.1.call-start = ((), (), s32[]{:S(2)}) async-start(), calls=%async_computation.30 | async-start | bytes 1310720 | tf_op jit(solution)/shard_map/all_gather | solution.py:102
  787.6 56.5 %reduce-scatter.51.cloned.1.call-start = ((), (), s32[]{:S(2)}) async-start(), calls=%async_computation.31 | async-start | bytes 1310720 | tf_op jit(solution)/shard_map/reduce_scatter | solution.py:115
  819.2 77.2 %all-gather.53.cloned.1.call-start = ((), (), s32[]{:S(2)}) async-start(), calls=%async_computation.43 | async-start | bytes 2359296 | tf_op jit(solution)/shard_map/all_gather | solution.py:229
  819.8 93.7 %all-gather.39.cloned.1.call-start = ((), (), s32[]{:S(2)}) async-start(), calls=%async_computation.32 | async-start | bytes 1310720 | tf_op jit(solution)/shard_map/all_gather | solution.py:102
  847.3 99.5 %reduce-scatter.53.cloned.1.call-start = ((), (), s32[]{:S(2)}) async-start(), calls=%async_computation.33 | async-start | bytes 1310720 | tf_op jit(solution)/shard_map/reduce_scatter | solution.py:115
  921.9 45.0 %copy-start.8 = (bf16[1,256,1024]{2,1,0:T(8,128)(2,1)S(1)}, bf16[1,256,1024]{2,1,0:T(8,128)(2,1)}, u32[]{:S(2)}) copy-start(bf16[1,256,1024]{2,1,0:T(8,128)(2,1)} %copy-done.7) | copy-start | bytes 1572868
  921.9 45.0 %copy-start.14 = (bf16[4,64,512]{2,1,0:T(8,128)(2,1)S(1)}, bf16[4,64,512]{2,1,0:T(8,128)(2,1)}, u32[]{:S(2)}) copy-start(bf16[4,64,512]{2,1,0:T(8,128)(2,1)} %copy-done.13) | copy-start | bytes 786436
  921.9 45.0 %all-gather.41.cloned.1.call-start = ((), (), s32[]{:S(2)}) async-start(), calls=%async_computation.34 | async-start | bytes 1310720 | tf_op jit(solution)/shard_map/all_gather | solution.py:102
  950.0 64.5 %reduce-scatter.55.cloned.1.call-start = ((), (), s32[]{:S(2)}) async-start(), calls=%async_computation.35 | async-start | bytes 1310720 | tf_op jit(solution)/shard_map/reduce_scatter | solution.py:115
  979.0 97.6 %reduce-scatter.75.cloned.1.call-start = ((), (), s32[]{:S(2)}) async-start(), calls=%async_computation.51 | async-start | bytes 2359296
  985.2 156.2 %reduce-scatter.67.cloned.1.call-start = ((), (), s32[]{:S(2)}) async-start(), calls=%async_computation.47 | async-start | bytes 73728
  986.2 220.9 %reduce-scatter.71.cloned.1.call-start = ((), (), s32[]{:S(2)}) async-start(), calls=%async_computation.49 | async-start | bytes 589824
  988.0 286.9 %reduce-scatter.63.cloned.1.call-start = ((), (), s32[]{:S(2)}) async-start(), calls=%async_computation.45 | async-start | bytes 1769472
  996.1 343.9 %reduce-scatter.65.cloned.1.call-start = ((), (), s32[]{:S(2)}) async-start(), calls=%async_computation.46 | async-start | bytes 73728
  997.1 413.7 %reduce-scatter.73.cloned.1.call-start = ((), (), s32[]{:S(2)}) async-start(), calls=%async_computation.50 | async-start | bytes 2359296
  1003.3 478.4 %reduce-scatter.59.cloned.1.call-start = ((), (), s32[]{:S(2)}) async-start(), calls=%async_computation.37 | async-start | bytes 2359296 | tf_op jit(solution)/shard_map/reduce_scatter | solution.py:291
  1007.5 544.9 %reduce-scatter.57.cloned.1.call-start = ((), (), s32[]{:S(2)}) async-start(), calls=%async_computation.36 | async-start | bytes 2359296 | tf_op jit(solution)/shard_map/reduce_scatter | solution.py:291
  1011.7 606.4 %reduce-scatter.69.cloned.1.call-start = ((), (), s32[]{:S(2)}) async-start(), calls=%async_computation.48 | async-start | bytes 589824
  1014.4 740.6 %reduce-scatter.77.cloned.1.call-start = ((), (), s32[]{:S(2)}) async-start(), calls=%async_computation.52 | async-start | bytes 540672
  1017.8 871.1 %reduce-scatter.79.cloned.1.call-start = ((), (), s32[]{:S(2)}) async-start(), calls=%async_computation.53 | async-start | bytes 540672
  1019.9 934.0 %reduce-scatter.61.cloned.1.call-start = ((), (), s32[]{:S(2)}) async-start(), calls=%async_computation.44 | async-start | bytes 1769472
  1410.9 208.9 %copy-start.12 = (bf16[128,1024]{1,0:T(8,128)(2,1)S(1)}, bf16[128,1024]{1,0:T(8,128)(2,1)}, u32[]{:S(2)}) copy-start(bf16[128,1024]{1,0:T(8,128)(2,1)} %reduce-scatter.55.cloned.1.call-done) | copy-start | bytes 786436
  (41 other events, 172.6 us)
Sparse Core Ops, SparseCore 0:
  149.3 14.1 all-gather.26
  166.1 45.3 all-gather.42
  257.1 30.7 reduce-scatter.40
  290.4 81.8 all-gather.44
  374.3 20.4 all-gather.28
  406.4 31.1 reduce-scatter.42
  440.3 46.9 all-gather.46
  489.4 14.8 all-gather.30
  513.3 31.1 reduce-scatter.44
  547.0 53.0 all-gather.48
  602.2 16.8 all-gather.32
  620.5 16.6 all-gather.34
  639.9 50.3 all-gather.50
  698.8 22.9 reduce-scatter.48
  754.2 30.4 reduce-scatter.46
  787.7 16.6 all-gather.36
  819.3 24.7 reduce-scatter.50
  846.0 50.3 all-gather.52
  898.5 14.8 all-gather.38
  922.0 24.7 reduce-scatter.52
  950.1 16.6 all-gather.40
  979.1 24.8 reduce-scatter.54
  1007.5 69.0 reduce-scatter.74
  1079.9 61.4 reduce-scatter.66
  1145.3 61.6 reduce-scatter.70
  1210.3 64.5 reduce-scatter.62
  1278.7 61.2 reduce-scatter.64
  1343.5 67.3 reduce-scatter.72
  1414.4 67.2 reduce-scatter.58
  1485.1 67.2 reduce-scatter.56
  1556.3 61.7 reduce-scatter.68
  1620.3 134.6 reduce-scatter.76
  1757.1 131.6 reduce-scatter.78
  1892.3 61.5 reduce-scatter.60
